TPU v7x, 32 devices: a whole 2x2x4 slice. The times are simulated.
32 devices in a mesh: dom: 8 (over z, y), mp: 4 (over x, core).
Axes of the slice: x: 2, y: 2, z: 4, core: 2. Of those that a mesh axis runs over, the one named last changes fastest.
Arguments:
- grid_feat: bfloat16 [32768, 256], P(('dom', 'mp')), may hold values from -6 to 6
- grid_target: int32 [32768], P(('dom', 'mp')), may hold values from 0 to 8191, as said below
- enc_w1: bfloat16 [256, 512], replicated, may hold values from -0.375 to 0.375
- enc_b1: float32 [512], replicated, may hold values from -3 to 3
- enc_w2: bfloat16 [512, 512], replicated, may hold values from -0.25 to 0.25
- enc_gain: float32 [512], replicated, may hold values from 0.25 to 1.75
- mesh_embed: bfloat16 [8192, 512], P('dom', 'mp'), may hold values from -6 to 6
- nbr_blocks: int32 [128, 16], P('dom'), may hold values from 0 to 127, as said below
- attn_bias: float32 [8, 16, 8192], P('mp', None, 'dom'), may hold values from -2 to 300
- ln_gain: float32 [2, 2, 512], replicated, may hold values from 0.25 to 1.75
- qkv_w: bfloat16 [2, 3, 512, 512], P(None, None, None, 'mp'), may hold values from -0.25 to 0.25
- out_w: bfloat16 [2, 512, 512], P(None, 'mp'), may hold values from -0.25 to 0.25
- up_w: bfloat16 [2, 512, 2048], P(None, None, 'mp'), may hold values from -0.25 to 0.25
- down_w: bfloat16 [2, 2048, 512], P(None, 'mp'), may hold values from -0.125 to 0.125
Outputs:
- mesh_out: bfloat16 [8192, 512], P('dom', 'mp')
Inputs may be any that keep to these rules, and one draw needn't show every extreme that they name: `grid_target`: among the 1024 grid nodes of one device (devices in the order dom, then mp), at most 256 have targets among the mesh nodes e * 1024 to (e + 1) * 1024 - 1 of one dom index e, and in every draw some dom index receives exactly 256 from every device. `nbr_blocks`: row b lists 16 different blocks, b itself among them, all within the 24 blocks that start at (b // 16) * 16 - 4, counted around the cycle of 128 blocks.
All inputs are finite; a program needn't handle non-finite values.
Results may differ from a plain program's by a relative error of at most 0.014.
Values may be sent and summed in bfloat16 or wider, within the bound.
A program may use at most 128 MiB of HBM per device.

v0:
```python
import jax
import jax.numpy as jnp
from jax import lax
from jax.sharding import PartitionSpec as P

HEAD_DIM = 64
BLK = 64
NBLK = 16
HB = 4


EPS = 1e-05


def with_halo(cells, sides, width):
    for axis, dim in sides:
        count = lax.axis_size(axis)
        head = lax.slice_in_dim(cells, 0, width, axis=dim)
        tail = lax.slice_in_dim(cells, cells.shape[dim] - width, cells.shape[dim], axis=dim)
        cells = jnp.concatenate(
            [
                lax.ppermute(tail, axis, [(i, (i + 1) % count) for i in range(count)]),
                cells,
                lax.ppermute(head, axis, [((i + 1) % count, i) for i in range(count)]),
            ],
            axis=dim,
        )
    return cells


def normalize(values, gain_vector):
    values = values.astype(jnp.float32)
    row_mean = jnp.mean(values, axis=-1, keepdims=True)
    centered = values - row_mean
    variance = jnp.mean(centered * centered, axis=-1, keepdims=True)
    return centered * lax.rsqrt(variance + EPS) * gain_vector


def encode(features, enc_w1, enc_b1, enc_w2, enc_gain):
    first = jnp.dot(features, enc_w1, preferred_element_type=jnp.float32) + enc_b1
    first = jax.nn.silu(first).astype(jnp.bfloat16)
    second = jnp.dot(first, enc_w2, preferred_element_type=jnp.float32)
    return normalize(second, enc_gain).astype(jnp.bfloat16)


def keep_rows(stream):
    return stream


def combine_all(partial_value):
    return lax.psum(partial_value.astype(jnp.bfloat16), "mp").astype(jnp.float32)


def attention(normed, qkv_layer, nbr_blocks, attn_bias):
    columns = qkv_layer.shape[2]
    mesh_nodes = normed.shape[0]
    local_blocks = mesh_nodes // BLK
    heads_here = columns // HEAD_DIM
    projected = jnp.einsum(
        "md,cde->cme", normed, qkv_layer, preferred_element_type=jnp.float32
    ).astype(jnp.bfloat16)
    key_value = jnp.concatenate([projected[1], projected[2]], axis=1)
    widened = with_halo(key_value, (("dom", 0),), HB * BLK)
    windowed = widened.reshape(local_blocks + 2 * HB, BLK, 2 * columns)
    window_start = lax.axis_index("dom") * local_blocks - HB
    window_slots = (nbr_blocks - window_start) % (local_blocks * lax.axis_size("dom"))
    picked = windowed[window_slots]
    key_rows = picked[..., :columns].reshape(local_blocks, NBLK * BLK, heads_here, HEAD_DIM)
    value_rows = picked[..., columns:].reshape(local_blocks, NBLK * BLK, heads_here, HEAD_DIM)
    queries = projected[0].reshape(local_blocks, BLK, heads_here, HEAD_DIM)
    scores = jnp.einsum(
        "tqhe,tkhe->thqk", queries, key_rows, preferred_element_type=jnp.float32
    ) * HEAD_DIM ** (-0.5)
    bias_rows = jnp.transpose(attn_bias.reshape(heads_here, NBLK, local_blocks, BLK), (2, 0, 3, 1))
    scores = scores.reshape(local_blocks, heads_here, BLK, NBLK, BLK) + bias_rows[..., None]
    row_max = jnp.max(scores, axis=(3, 4), keepdims=True)
    exponent = jnp.exp(scores - row_max)
    weights = (exponent / jnp.sum(exponent, axis=(3, 4), keepdims=True)).astype(jnp.bfloat16)
    weights = weights.reshape(local_blocks, heads_here, BLK, NBLK * BLK)
    attended = jnp.einsum(
        "thqk,tkhe->tqhe", weights, value_rows, preferred_element_type=jnp.float32
    )
    return attended.astype(jnp.bfloat16).reshape(mesh_nodes, columns)


def layer_step(
    stream,
    layer_index,
    widen_fn,
    reduce_fn,
    ln_gain,
    qkv_w,
    out_w,
    up_w,
    down_w,
    nbr_blocks,
    attn_bias,
):
    full_rows = widen_fn(stream)
    normed = normalize(full_rows, ln_gain[layer_index, 0]).astype(jnp.bfloat16)
    attended = attention(normed, qkv_w[layer_index], nbr_blocks, attn_bias)
    partial_value = jnp.dot(attended, out_w[layer_index], preferred_element_type=jnp.float32)
    stream = (stream.astype(jnp.float32) + reduce_fn(partial_value)).astype(jnp.bfloat16)
    full_rows = widen_fn(stream)
    normed = normalize(full_rows, ln_gain[layer_index, 1]).astype(jnp.bfloat16)
    hidden = jax.nn.silu(
        jnp.dot(normed, up_w[layer_index], preferred_element_type=jnp.float32)
    ).astype(jnp.bfloat16)
    partial_value = jnp.dot(hidden, down_w[layer_index], preferred_element_type=jnp.float32)
    return (stream.astype(jnp.float32) + reduce_fn(partial_value)).astype(jnp.bfloat16)


def shards(
    grid_feat,
    grid_target,
    enc_w1,
    enc_b1,
    enc_w2,
    enc_gain,
    mesh_embed,
    nbr_blocks,
    attn_bias,
    ln_gain,
    qkv_w,
    out_w,
    up_w,
    down_w,
):
    dom_count = lax.axis_size("dom")
    mp_count = lax.axis_size("mp")
    grid_rows = grid_feat.shape[0]
    full_width = enc_w2.shape[1]
    columns = full_width // mp_count
    mesh_nodes = mesh_embed.shape[0]
    capacity = 2 * grid_rows // dom_count
    message = encode(grid_feat, enc_w1, enc_b1, enc_w2, enc_gain)
    owner_dom = grid_target // mesh_nodes
    target_node = grid_target % mesh_nodes
    member_of = (owner_dom[:, None] == jnp.arange(dom_count, dtype=jnp.int32)[None, :]).astype(
        jnp.int32
    )
    count_before = jnp.cumsum(member_of, axis=0) - member_of
    rank_within = jnp.sum(count_before * member_of, axis=1)
    slot_index = owner_dom * capacity + rank_within
    source_row = (
        jnp.full((dom_count * capacity,), grid_rows, jnp.int32)
        .at[slot_index]
        .set(jnp.arange(grid_rows, dtype=jnp.int32))
    )
    padded = jnp.concatenate([message, jnp.zeros((1, full_width), jnp.bfloat16)], axis=0)
    outgoing = padded[source_row].reshape(dom_count, capacity, mp_count, columns)
    landing = jnp.concatenate([target_node, jnp.zeros((1,), jnp.int32)])[source_row].reshape(
        dom_count, capacity, 1
    )
    landing = jnp.broadcast_to(landing, (dom_count, capacity, mp_count))
    direct_rows = jnp.transpose(outgoing, (0, 2, 1, 3)).reshape(
        dom_count * mp_count, capacity, columns
    )
    direct_index = jnp.transpose(landing, (0, 2, 1)).reshape(dom_count * mp_count, capacity)
    received, arrivals = (
        lax.all_to_all(direct_rows, ("dom", "mp"), split_axis=0, concat_axis=0, tiled=True),
        lax.all_to_all(direct_index, ("dom", "mp"), split_axis=0, concat_axis=0, tiled=True),
    )
    received = received.reshape(-1, columns)
    arrivals = arrivals.reshape(-1)
    gathered = jax.ops.segment_sum(received.astype(jnp.float32), arrivals, num_segments=mesh_nodes)
    stream = (mesh_embed.astype(jnp.float32) + gathered).astype(jnp.bfloat16)
    stream = lax.all_gather(stream, "mp", axis=1, tiled=True)
    for layer_index in range(ln_gain.shape[0]):
        stream = layer_step(
            stream,
            layer_index,
            keep_rows,
            combine_all,
            ln_gain,
            qkv_w,
            out_w,
            up_w,
            down_w,
            nbr_blocks,
            attn_bias,
        )
    return lax.dynamic_slice_in_dim(stream, lax.axis_index("mp") * columns, columns, 1)


def solution(mesh):
    placed = (
        P(("dom", "mp"), None),
        P(("dom", "mp")),
        P(),
        P(),
        P(),
        P(),
        P("dom", "mp"),
        P("dom", None),
        P("mp", None, "dom"),
        P(),
        P(None, None, None, "mp"),
        P(None, "mp", None),
        P(None, None, "mp"),
        P(None, "mp", None),
    )
    return jax.shard_map(
        shards, mesh=mesh, in_specs=placed, out_specs=P("dom", "mp"), check_vma=False
    )
```

profile of v0, /device:TPU:13, one launch (start us, length us, event | category | flops | bytes accessed | tf_op | source)
XLA Modules:
  0.0 534.3 jit_solution(8785928098901920885)
XLA Ops:
  14.5 11.8 %gather_fusion = s32[2048]{0:T(1024)S(1)} fusion(s32[1025]{0:T(1024)S(1)} %pad_add_fusion, s32[2048]{0:T(1024)S(1)} %fusion.106), kind=kCustom, calls=%fused_computation | custom fusion | bytes 24576 | tf_op jit(solution)/shard_map/gather | solution.py:152
  27.0 6.3 %all-to-all-start = ((s32[32,1,256]{2,1,0:T(1,128)}), s32[32,1,256]{2,1,0:T(1,128)S(1)}, u32[]{:S(2)}, u32[]{:S(2)}) async-start(s32[32,1,256]{2,1,0:T(1,128)} %all_to_all.9), calls=%async_computation | async-start | bytes 65536 | tf_op jit(solution)/shard_map/all_to_all | solution.py:162
  36.6 9.2 %gather_fusion.1 = bf16[2048,512]{1,0:T(8,128)(2,1)} fusion(bf16[1025,512]{1,0:T(8,128)(2,1)S(1)} %concatenate.19, s32[2048]{0:T(1024)S(1)} %fusion.106), kind=kCustom, calls=%fused_computation.1 | custom fusion | bytes 4202496 | tf_op jit(solution)/shard_map/gather | solution.py:151
  57.2 44.5 %all-to-all-done.1 = bf16[32,256,128]{2,1,0:T(8,128)(2,1)S(1)} async-done(((bf16[32,256,128]{2,1,0:T(8,128)(2,1)}), bf16[32,256,128]{2,1,0:T(8,128)(2,1)S(1)}, u32[]{:S(2)}, u32[]{:S(2)}) %all-to-all-start.1) | async-done | bytes 2097184 | tf_op jit(solution)/shard_map/all_to_all | solution.py:161
  101.7 51.4 %scatter_custom_fusion.1 = f32[1024,128]{1,0:T(8,128)S(1)} fusion(f32[1024,128]{1,0:T(8,128)S(1)} %convert_element_type.127, s32[8192]{0:T(1024)S(1)} %bitcast.128, bf16[8192,128]{1,0:T(8,128)(2,1)S(1)} %bitcast.119), kind=kCustom, calls=%fused_computation.22 | custom fusion | flops 2097152 | bytes 2621440 | tf_op jit(solution)/shard_map/scatter-add | solution.py:166
  155.5 17.7 %all-gather.2.cloned.1.call-done = bf16[1024,512]{1,0:T(8,128)(2,1)} async-done(((bf16[1024,128]{1,0:T(8,128)(2,1)}), bf16[1024,512]{1,0:T(8,128)(2,1)}) %all-gather.2.cloned.1.call-update) | async-done | bytes 1048592 | tf_op jit(solution)/shard_map/all_gather | solution.py:168
  181.4 8.5 %add.154 = f32[16,2,64,16,64]{4,3,2,1,0:T(8,128)} broadcast(f32[16,2,64,16]{3,2,1,0:T(8,128)S(1)} %copy.45), dimensions={0,1,2,3} | broadcast | bytes 8519680 | tf_op jit(solution)/shard_map/add | solution.py:75
  189.9 14.5 %add.155 = f32[16,2,64,1024]{3,2,1,0:T(8,128)} reshape(f32[16,2,64,16,64]{4,3,2,1,0:T(8,128)} %add.154) | data formatting | bytes 16777216 | tf_op jit(solution)/shard_map/add | solution.py:75
  206.0 8.6 %gather_fusion.2 = bf16[256,64,256]{2,1,0:T(8,128)(2,1)} fusion(bf16[24,64,256]{2,1,0:T(8,128)(2,1)S(1)} %bitcast.116, s32[1024]{0:T(1024)S(1)} %pad_clamp_fusion), kind=kCustom, calls=%fused_computation.2 | custom fusion | bytes 16778240 | tf_op jit(solution)/shard_map/gather | solution.py:67
  214.6 6.9 %fusion.120 = (bf16[16,16,64,128]{3,2,1,0:T(8,128)(2,1)}, bf16[16,16,64,128]{3,2,1,0:T(8,128)(2,1)}) fusion(bf16[16,16,64,256]{3,2,1,0:T(8,128)(2,1)} %bitcast.118), kind=kLoop, calls=%fused_computation.163 | loop fusion | bytes 16777216 | tf_op jit(solution)/shard_map/slice | solution.py:69
  221.5 14.8 %reshape.216 = bf16[16,1024,2,64]{3,2,1,0:T(2,128)(2,1)} reshape(bf16[16,16,64,128]{3,2,1,0:T(8,128)(2,1)} %get-tuple-element.14) | data formatting | bytes 8388608 | tf_op jit(solution)/shard_map/reshape | solution.py:68
  236.3 8.8 %multiply_add_fusion.1 = f32[16,2,64,1024]{3,2,1,0:T(8,128)S(1)} fusion(f32[16,2,64,1024]{3,2,1,0:T(8,128)} %add.155, bf16[16,1024,2,64]{3,2,1,0:T(2,128)(2,1)} %reshape.216, bf16[16,64,2,64]{1,0,3,2:T(8,128)(2,1)S(1)} %copy-done.8), kind=kOutput, calls=%fused_computation.21 | convolution fusion | flops 272629760 | bytes 21233664 | tf_op jit(solution)/shard_map/tqhe,tkhe->thqk/dot_general | solution.py:71
  248.3 14.8 %reshape.215 = bf16[16,1024,2,64]{3,2,1,0:T(2,128)(2,1)} reshape(bf16[16,16,64,128]{3,2,1,0:T(8,128)(2,1)} %get-tuple-element.13) | data formatting | bytes 8388608 | tf_op jit(solution)/shard_map/reshape | solution.py:69
  263.2 14.1 %fusion.46 = bf16[16,64,2,64]{1,3,2,0:T(8,128)(2,1)S(1)} fusion(f32[16,2,64]{2,1,0:T(2,128)S(1)} %fusion.126, bf16[16,1024,2,64]{3,2,1,0:T(2,128)(2,1)} %reshape.215, f32[16,2,64,1024]{3,2,1,0:T(8,128)} %copy-done.3), kind=kOutput, calls=%fused_computation.69 | convolution fusion | flops 274861056 | bytes 12853248 | tf_op jit(solution)/shard_map/thqk,tkhe->tqhe/dot_general | solution.py:80
  279.5 37.7 %all-reduce.6.cloned.1.call-done = bf16[1024,512]{1,0:T(8,128)(2,1)} async-done(((bf16[1024,512]{1,0:T(8,128)(2,1)}), bf16[1024,512]{1,0:T(8,128)(2,1)}) %all-reduce.6.cloned.1.call-update) | async-done | bytes 1048592 | tf_op jit(solution)/shard_map/psum | solution.py:51
  323.5 36.7 %all-reduce.8.cloned.1.call-done = bf16[1024,512]{1,0:T(8,128)(2,1)} async-done(((bf16[1024,512]{1,0:T(8,128)(2,1)}), bf16[1024,512]{1,0:T(8,128)(2,1)}) %all-reduce.8.cloned.1.call-update) | async-done | bytes 1048592 | tf_op jit(solution)/shard_map/psum | solution.py:51
  371.9 8.6 %gather_fusion.3 = bf16[256,64,256]{2,1,0:T(8,128)(2,1)} fusion(bf16[24,64,256]{2,1,0:T(8,128)(2,1)S(1)} %bitcast.115, s32[1024]{0:T(1024)S(1)} %pad_clamp_fusion), kind=kCustom, calls=%fused_computation.3 | custom fusion | bytes 16778240 | tf_op jit(solution)/shard_map/gather | solution.py:67
  380.5 6.9 %fusion.119 = (bf16[16,16,64,128]{3,2,1,0:T(8,128)(2,1)}, bf16[16,16,64,128]{3,2,1,0:T(8,128)(2,1)}) fusion(bf16[16,16,64,256]{3,2,1,0:T(8,128)(2,1)} %bitcast.117), kind=kLoop, calls=%fused_computation.162 | loop fusion | bytes 16777216 | tf_op jit(solution)/shard_map/slice | solution.py:69
  387.4 14.8 %reshape.218 = bf16[16,1024,2,64]{3,2,1,0:T(2,128)(2,1)} reshape(bf16[16,16,64,128]{3,2,1,0:T(8,128)(2,1)} %get-tuple-element.12) | data formatting | bytes 8388608 | tf_op jit(solution)/shard_map/reshape | solution.py:68
  402.2 8.8 %multiply_add_fusion = f32[16,2,64,1024]{3,2,1,0:T(8,128)S(1)} fusion(f32[16,2,64,1024]{3,2,1,0:T(8,128)} %add.155, bf16[16,1024,2,64]{3,2,1,0:T(2,128)(2,1)} %reshape.218, bf16[16,64,2,64]{1,0,3,2:T(8,128)(2,1)S(1)} %copy-done.7), kind=kOutput, calls=%fused_computation.18 | convolution fusion | flops 272629760 | bytes 21233664 | tf_op jit(solution)/shard_map/tqhe,tkhe->thqk/dot_general | solution.py:71
  414.2 14.9 %reshape.217 = bf16[16,1024,2,64]{3,2,1,0:T(2,128)(2,1)} reshape(bf16[16,16,64,128]{3,2,1,0:T(8,128)(2,1)} %get-tuple-element.11) | data formatting | bytes 8388608 | tf_op jit(solution)/shard_map/reshape | solution.py:69
  429.2 14.1 %fusion.43 = bf16[16,64,2,64]{1,3,2,0:T(8,128)(2,1)S(1)} fusion(f32[16,2,64]{2,1,0:T(2,128)S(1)} %fusion.127, bf16[16,1024,2,64]{3,2,1,0:T(2,128)(2,1)} %reshape.217, f32[16,2,64,1024]{3,2,1,0:T(8,128)} %copy-done.2), kind=kOutput, calls=%fused_computation.68 | convolution fusion | flops 274861056 | bytes 12853248 | tf_op jit(solution)/shard_map/thqk,tkhe->tqhe/dot_general | solution.py:80
  445.5 37.2 %all-reduce.10.cloned.1.call-done = bf16[1024,512]{1,0:T(8,128)(2,1)} async-done(((bf16[1024,512]{1,0:T(8,128)(2,1)}), bf16[1024,512]{1,0:T(8,128)(2,1)}) %all-reduce.10.cloned.1.call-update) | async-done | bytes 1048592 | tf_op jit(solution)/shard_map/psum | solution.py:51
  490.2 35.2 %all-reduce.12.cloned.1.call-done = bf16[1024,512]{1,0:T(8,128)(2,1)} async-done(((bf16[1024,512]{1,0:T(8,128)(2,1)}), bf16[1024,512]{1,0:T(8,128)(2,1)}) %all-reduce.12.cloned.1.call-update) | async-done | bytes 1048592 | tf_op jit(solution)/shard_map/psum | solution.py:51
  (136 shorter events, 73.4 us)
Async XLA Ops:
  6.5 26.7 %copy-start = (bf16[512,512]{1,0:T(8,128)(2,1)S(1)}, bf16[512,512]{1,0:T(8,128)(2,1)}, u32[]{:S(2)}) copy-start(bf16[512,512]{1,0:T(8,128)(2,1)} %param.18) | copy-start | bytes 1572868
  14.5 18.8 %copy-start.18 = (bf16[1024,256]{1,0:T(8,128)(2,1)S(1)}, bf16[1024,256]{1,0:T(8,128)(2,1)}, u32[]{:S(2)}) copy-start(bf16[1024,256]{1,0:T(8,128)(2,1)} %param.14) | copy-start | bytes 1572868
  14.5 18.8 %copy-start.19 = (f32[512]{0:T(512)S(1)}, f32[512]{0:T(512)}, u32[]{:S(2)}) copy-start(f32[512]{0:T(512)} %param.17) | copy-start | bytes 6148
  27.0 23.2 %all-to-all-start = ((s32[32,1,256]{2,1,0:T(1,128)}), s32[32,1,256]{2,1,0:T(1,128)S(1)}, u32[]{:S(2)}, u32[]{:S(2)}) async-start(s32[32,1,256]{2,1,0:T(1,128)} %all_to_all.9), calls=%async_computation | async-start | bytes 65536 | tf_op jit(solution)/shard_map/all_to_all | solution.py:162
  50.2 51.4 %all-to-all-start.1 = ((bf16[32,256,128]{2,1,0:T(8,128)(2,1)}), bf16[32,256,128]{2,1,0:T(8,128)(2,1)S(1)}, u32[]{:S(2)}, u32[]{:S(2)}) async-start(bf16[32,256,128]{2,1,0:T(8,128)(2,1)} %bitcast.120), calls=%async_computation.1 | async-start | bytes 4194304 | tf_op jit(solution)/shard_map/all_to_all | solution.py:161
  56.0 97.8 %copy-start.10 = (bf16[2,3,512,128]{3,2,1,0:T(8,128)(2,1)S(1)}, bf16[2,3,512,128]{3,2,1,0:T(8,128)(2,1)}, u32[]{:S(2)}) copy-start(bf16[2,3,512,128]{3,2,1,0:T(8,128)(2,1)} %param.24) | copy-start | bytes 2359300
  56.1 117.1 %all-gather.2.cloned.1.call-start = ((), (), s32[]{:S(2)}) async-start(), calls=%async_computation.2 | async-start | bytes 1310720 | tf_op jit(solution)/shard_map/all_gather | solution.py:168
  153.8 163.5 %all-reduce.6.cloned.1.call-start = ((), (), s32[]{:S(2)}) async-start(), calls=%async_computation.3 | async-start | bytes 2097152 | tf_op jit(solution)/shard_map/psum | solution.py:51
  178.1 27.5 %collective-permute-start.1 = (bf16[256,256]{0,1:T(8,128)(2,1)}, bf16[256,256]{0,1:T(8,128)(2,1)S(1)}, u32[]{:S(2)}, u32[]{:S(2)}) collective-permute-start(bf16[256,256]{0,1:T(8,128)(2,1)} %get-tuple-element.26), channel_id=1, source_target_pairs={{4,0},{8,4},{12,8},{16,12},{20,16},{24,20},{28,24},{0,28},{5,1},{9... | collective-permute-start | bytes 393224 | tf_op jit(solution)/shard_map/ppermute | solution.py:24
  178.4 27.3 %collective-permute-start = (bf16[256,256]{0,1:T(8,128)(2,1)}, bf16[256,256]{0,1:T(8,128)(2,1)S(1)}, u32[]{:S(2)}, u32[]{:S(2)}) collective-permute-start(bf16[256,256]{0,1:T(8,128)(2,1)} %get-tuple-element.25), channel_id=1, source_target_pairs={{0,4},{4,8},{8,12},{12,16},{16,20},{20,24},{24,28},{28,0},{1,5},{5... | collective-permute-start | bytes 393224 | tf_op jit(solution)/shard_map/ppermute | solution.py:22
  221.5 14.8 %copy-start.8 = (bf16[16,64,2,64]{1,0,3,2:T(8,128)(2,1)S(1)}, bf16[16,64,2,64]{1,0,3,2:T(8,128)(2,1)}, u32[]{:S(2)}) copy-start(bf16[16,64,2,64]{1,0,3,2:T(8,128)(2,1)} %reshape_squeeze.6) | copy-start | bytes 786436
  263.2 14.8 %copy-start.11 = (bf16[2,128,512]{2,1,0:T(8,128)(2,1)S(1)}, bf16[2,128,512]{2,1,0:T(8,128)(2,1)}, u32[]{:S(2)}) copy-start(bf16[2,128,512]{2,1,0:T(8,128)(2,1)} %param.25) | copy-start | bytes 786436
  279.5 40.0 %copy-start.16 = (f32[1,1,512]{2,1,0:T(1,128)S(1)}, f32[1,1,512]{2,1,0:T(1,128)}, u32[]{:S(2)}) copy-start(f32[1,1,512]{2,1,0:T(1,128)} %get-tuple-element.28) | copy-start | bytes 6148
  279.5 80.6 %all-reduce.8.cloned.1.call-start = ((), (), s32[]{:S(2)}) async-start(), calls=%async_computation.4 | async-start | bytes 2097152 | tf_op jit(solution)/shard_map/psum | solution.py:51
  318.9 4.3 copy-start.5
  319.5 3.8 copy-start.9
  323.2 37.0 %copy-start.6 = (bf16[1024,512]{1,0:T(8,128)(2,1)S(1)}, bf16[1024,512]{1,0:T(8,128)(2,1)}, u32[]{:S(2)}) copy-start(bf16[1024,512]{1,0:T(8,128)(2,1)} %copy-done.5) | copy-start | bytes 3145732
  323.2 159.5 %all-reduce.10.cloned.1.call-start = ((), (), s32[]{:S(2)}) async-start(), calls=%async_computation.5 | async-start | bytes 2097152 | tf_op jit(solution)/shard_map/psum | solution.py:51
  363.3 4.9 collective-permute-start.3
  363.6 7.9 %collective-permute-start.2 = (bf16[256,256]{0,1:T(8,128)(2,1)S(1)}, bf16[256,256]{0,1:T(8,128)(2,1)S(1)}, u32[]{:S(2)}, u32[]{:S(2)}) collective-permute-start(bf16[256,256]{0,1:T(8,128)(2,1)S(1)} %get-tuple-element.23), channel_id=1, source_target_pairs={{0,4},{4,8},{8,12},{12,16},{16,20},{20,24},{24,28},{28,0},{1,5},{5... | collective-permute-start | bytes 393224 | tf_op jit(solution)/shard_map/ppermute | solution.py:22
  387.4 14.8 %copy-start.7 = (bf16[16,64,2,64]{1,0,3,2:T(8,128)(2,1)S(1)}, bf16[16,64,2,64]{1,0,3,2:T(8,128)(2,1)}, u32[]{:S(2)}) copy-start(bf16[16,64,2,64]{1,0,3,2:T(8,128)(2,1)} %reshape_squeeze.7) | copy-start | bytes 786436
  429.1 14.8 %copy-start.12 = (bf16[2,128,512]{2,1,0:T(8,128)(2,1)S(1)}, bf16[2,128,512]{2,1,0:T(8,128)(2,1)}, u32[]{:S(2)}) copy-start(bf16[2,128,512]{2,1,0:T(8,128)(2,1)} %param.25) | copy-start | bytes 786436
  445.5 80.0 %all-reduce.12.cloned.1.call-start = ((), (), s32[]{:S(2)}) async-start(), calls=%async_computation.6 | async-start | bytes 2097152 | tf_op jit(solution)/shard_map/psum | solution.py:51
  488.5 38.8 %copy-start.1 = (bf16[512,512]{1,0:T(8,128)(2,1)S(1)}, bf16[512,512]{1,0:T(8,128)(2,1)}, u32[]{:S(2)}) copy-start(bf16[512,512]{1,0:T(8,128)(2,1)} %param.18) | copy-start | bytes 1572868
  (7 other events, 19.7 us)
Sparse Core Ops, SparseCore 0:
  153.9 19.1 all-gather.1
  279.6 37.6 all-reduce.5
  323.3 36.7 all-reduce.7
  445.6 37.0 all-reduce.9
  488.6 36.7 all-reduce.11
where the time goes:
time: 545 us; the launch traced here: 534 us
  waiting for transfers between devices  214 us (39%)
  local copies, waits for them, and re-layouts  154 us (28%)
  other arithmetic  75 us (14%)
  matrix products  60 us (11%)
  starting transfers between devices  17.7 us (3%)
  between operations  14.2 us (3%)
    psum x4, waiting for transfers between devices, combine_all(): lax.psum(partial_value.astype(jnp.bfloat16), 'mp').astype(jnp.float32)  147 us
    scatter-add x1, other arithmetic, shards(): jax.ops.segment_sum(received.astype(jnp.float32), arrivals, num_segments=...  51.4 us
    all_to_all x1, waiting for transfers between devices, shards(): lax.all_to_all(direct_rows, ('dom', 'mp'), split_axis=0, concat_axis=0, t...  44.5 us
    reshape x2, local copies, waits for them, and re-layouts, attention(): picked[..., columns:]  29.8 us
    reshape x2, local copies, waits for them, and re-layouts, attention(): picked[..., :columns]  29.5 us
    dot_general x2, matrix products, attention(): jnp.einsum('thqk,tkhe->tqhe', weights, value_rows, preferred_element_type...  28.2 us
    add x2, local copies, waits for them, and re-layouts, attention(): scores.reshape(local_blocks, heads_here, BLK, NBLK, BLK)  23 us
    dot_general x2, matrix products, attention(): jnp.einsum('tqhe,tkhe->thqk', queries, key_rows, preferred_element_type=j...  17.7 us
  transfers between devices with their start and end apart: 11, of which 8 were waited for; matrix products, arithmetic and copies ran while one was open for 9% of the time, Pallas kernels for 0%

commit v1 on v0

v1 whole, which is shorter than its diff:
```python
import functools

import jax
import jax.numpy as jnp
from jax import lax
from jax.experimental import pallas as pl
from jax.experimental.pallas import tpu as pltpu
from jax.sharding import PartitionSpec as P

HEAD_DIM = 64
BLK = 64
NBLK = 16
HB = 4
EPS = 1e-05
F32 = jnp.float32
BF16 = jnp.bfloat16
MESH = pl.DeviceIdType.MESH


def normalize(values, gain_row):
    row_mean = jnp.mean(values, axis=-1, keepdims=True)
    centered = values - row_mean
    variance = jnp.mean(centered * centered, axis=-1, keepdims=True)
    return centered * lax.rsqrt(variance + EPS) * gain_row


def silu(v):
    return v / (1.0 + jnp.exp(-v))


def mm(a, b):
    return jnp.dot(a, b, preferred_element_type=F32)


def mega(
    n_dom,
    n_mp,
    layers,
    slots,
    feat,
    target,
    w1,
    b1,
    w2,
    egain,
    embed,
    bias,
    ln_gain,
    qkv_w,
    out_w,
    up_w,
    down_w,
    result,
    sbuf,
    sland,
    rbuf,
    rland,
    acc,
    psend,
    precv,
    xrow,
    nrm,
    kv0,
    kv1,
    qs,
    att,
    arecv,
    gout,
    gup,
    gdown,
    d_send,
    d_recv,
    p_send,
    p_recv,
    ag_send,
    ag_recv,
    w_send,
    w_recv,
    h_send,
    h_recv,
    a_send,
    a_recv,
    f_send,
    f_recv,
):
    dom = lax.axis_index("dom")
    m = lax.axis_index("mp")
    rows = feat.shape[0]
    cap = sbuf.shape[1]
    nodes = embed.shape[0]
    cols = embed.shape[1]
    quarter = nodes // n_mp
    qblk = quarter // BLK
    heads = cols // HEAD_DIM
    local_blocks = nodes // BLK
    peers = [m + 1 - 2 * (m % 2), (m + 2) % 4, 3 - m]

    def dev(d, p):
        return (d, p)

    barrier = pltpu.get_barrier_semaphore()
    for k in range(1, n_dom):
        pl.semaphore_signal(barrier, inc=1, device_id=dev((dom + k) % n_dom, m), device_id_type=MESH)
    for p in peers:
        pl.semaphore_signal(barrier, inc=1, device_id=dev(dom, p), device_id_type=MESH)

    owner = target[...] // nodes
    node = target[...] % nodes
    row_e = lax.broadcasted_iota(jnp.int32, (n_dom, rows), 0)
    member = (row_e == owner).astype(F32)
    before = (
        lax.broadcasted_iota(jnp.int32, (rows, rows), 0)
        < lax.broadcasted_iota(jnp.int32, (rows, rows), 1)
    ).astype(F32).astype(BF16)
    count = mm(member.astype(BF16), before)
    rank = jnp.sum(count * member, axis=0, keepdims=True).astype(jnp.int32)
    slot = owner * cap + rank
    hi = (node // 32).astype(F32)
    lo = (node % 32).astype(F32)
    pick = lax.broadcasted_iota(jnp.int32, (16, rows), 0)
    parts = jnp.where(
        pick == 0, hi, jnp.where(pick == 1, lo, jnp.where(pick == 2, 1.0, 0.0))
    ).astype(BF16)
    features = feat[...]

    def outgoing(k):
        e = (dom + k) % n_dom
        here = (
            lax.broadcasted_iota(jnp.int32, (cap, rows), 0) == slot - e * cap
        ).astype(F32).astype(BF16)
        sbuf[k] = mm(here, features).astype(BF16)
        where_to = lax.dot_general(parts, here, (((1,), (1,)), ((), ())), preferred_element_type=F32)
        landed = where_to[0:1] * 32.0 + where_to[1:2]
        landed = jnp.where(where_to[2:3] > 0.5, landed, -1.0).astype(jnp.int32)
        sland[k] = jnp.broadcast_to(landed, (8, cap))

    def d_copies(k):
        target_dev = dev((dom + k) % n_dom, m)
        return (
            pltpu.make_async_remote_copy(
                sbuf.at[k], rbuf.at[k], d_send.at[0, k], d_recv.at[0, k],
                device_id=target_dev, device_id_type=MESH,
            ),
            pltpu.make_async_remote_copy(
                sland.at[k], rland.at[k], d_send.at[1, k], d_recv.at[1, k],
                device_id=target_dev, device_id_type=MESH,
            ),
        )

    order = sorted(range(1, n_dom), key=lambda k: -min(k, n_dom - k))
    outgoing(order[0])
    pl.semaphore_wait(barrier, n_dom - 1 + len(peers))
    started = {}

    def w_copies(layer, hop):
        out = []
        for i, (own, got) in enumerate(((out_w, gout), (up_w, gup), (down_w, gdown))):
            if hop < 2:
                src = own.at[layer]
                p = peers[hop]
            else:
                src = got.at[layer, 1]
                p = peers[0]
            out.append(
                pltpu.make_async_remote_copy(
                    src, got.at[layer, hop], w_send.at[layer, hop, i], w_recv.at[layer, hop, i],
                    device_id=dev(dom, p), device_id_type=MESH,
                )
            )
        return out

    wc = {(l, h): w_copies(l, h) for l in range(layers) for h in range(3)}

    def start_all(copies):
        for c in copies:
            c.start()

    for n, k in enumerate(order):
        if n:
            outgoing(k)
        started[k] = d_copies(k)
        start_all(started[k])
    start_all(wc[0, 1])
    start_all(wc[0, 0])
    outgoing(0)

    def consume(buf, land, first):
        v = mm(buf, w1[...]) + b1[...]
        message = normalize(mm(silu(v).astype(BF16), w2[...]), egain[...]).astype(BF16)
        scatter = (
            lax.broadcasted_iota(jnp.int32, (nodes, cap), 0) == land[0:1]
        ).astype(F32).astype(BF16)
        if first:
            acc[...] = mm(scatter, message)
        else:
            acc[...] += mm(scatter, message)

    consume(sbuf[0], sland[0], True)
    mine = pl.ds(pl.multiple_of(m * cols, cols), cols)
    acc[:, mine] += embed[...].astype(F32)
    for k in reversed(order):
        for c in started[k]:
            c.wait_recv()
        consume(rbuf[k], rland[k], False)

    def rows_of(p):
        return pl.ds(pl.multiple_of(p * quarter, quarter), quarter)

    pc = []
    for r in (2, 1, 0):
        psend[r] = acc[rows_of(peers[r]), :].astype(BF16)
        c = pltpu.make_async_remote_copy(
            psend.at[r], precv.at[r], p_send.at[r], p_recv.at[r],
            device_id=dev(dom, peers[r]), device_id_type=MESH,
        )
        c.start()
        pc.append(c)
    total = acc[rows_of(m), :]
    for c in reversed(pc):
        c.wait_recv()
    for r in range(3):
        total = total + precv[r].astype(F32)
    xrow[...] = total.astype(BF16)

    lane = lax.broadcasted_iota(jnp.int32, (BLK, cols), 1) // HEAD_DIM
    pending = []
    for layer in range(layers):
        kv = (kv0, kv1)[layer]
        nrm[layer, 3] = normalize(xrow[...].astype(F32), ln_gain[2 * layer : 2 * layer + 1, :]).astype(BF16)
        ag = []
        for r in range(3):
            c = pltpu.make_async_remote_copy(
                nrm.at[layer, 3], nrm.at[layer, r], ag_send.at[layer, r], ag_recv.at[layer, r],
                device_id=dev(dom, peers[r]), device_id_type=MESH,
            )
            ag.append(c)
        for r in (2, 1, 0):
            ag[r].start()
        if layer + 1 < layers:
            start_all(wc[layer + 1, 1])
            start_all(wc[layer + 1, 0])

        def project(r, p):
            block = nrm[layer, r]
            q = mm(block, qkv_w[layer, 0]).astype(BF16).astype(F32) * HEAD_DIM ** (-0.5)
            qs[layer, rows_of(p), :] = q.astype(BF16)
            spot = pl.ds(HB + p * qblk, qblk)
            kv[spot, :, 0:cols] = mm(block, qkv_w[layer, 1]).astype(BF16).reshape(qblk, BLK, cols)
            kv[spot, :, cols : 2 * cols] = (
                mm(block, qkv_w[layer, 2]).astype(BF16).reshape(qblk, BLK, cols)
            )

        project(3, m)
        for r in range(3):
            ag[r].wait_recv()
            project(r, peers[r])
        halo = [
            pltpu.make_async_remote_copy(
                kv.at[pl.ds(HB, HB)], kv.at[pl.ds(HB + local_blocks, HB)],
                h_send.at[layer, 0], h_recv.at[layer, 0],
                device_id=dev((dom + n_dom - 1) % n_dom, m), device_id_type=MESH,
            ),
            pltpu.make_async_remote_copy(
                kv.at[pl.ds(local_blocks, HB)], kv.at[pl.ds(0, HB)],
                h_send.at[layer, 1], h_recv.at[layer, 1],
                device_id=dev((dom + 1) % n_dom, m), device_id_type=MESH,
            ),
        ]
        start_all(halo)
        for c in wc[layer, 1]:
            c.wait_recv()
        start_all(wc[layer, 2])
        for c in halo:
            c.wait_recv()

        def attend(p):
            def body(i, carry):
                b = p * qblk + i
                span = pl.ds(pl.multiple_of(b * BLK, BLK), BLK)
                q = qs[layer, span, :]
                qbd = jnp.concatenate(
                    [jnp.where(lane == h, q.astype(F32), 0.0) for h in range(heads)], axis=0
                ).astype(BF16)
                picked = [kv[slots[b * NBLK + t]] for t in range(NBLK)]
                keys = jnp.concatenate([x[:, 0:cols] for x in picked], axis=0)
                values = jnp.concatenate([x[:, cols : 2 * cols] for x in picked], axis=0)
                s = lax.dot_general(keys, qbd, (((1,), (1,)), ((), ())), preferred_element_type=F32)
                s = s.reshape(NBLK, BLK, heads * BLK) + bias[b][:, None, :]
                s = s.reshape(NBLK * BLK, heads * BLK)
                e = jnp.exp(s - jnp.max(s, axis=0, keepdims=True))
                w = (e * (1.0 / jnp.sum(e, axis=0, keepdims=True))).astype(BF16)
                o = lax.dot_general(w, values, (((0,), (0,)), ((), ())), preferred_element_type=F32)
                merged = o[0:BLK]
                for h in range(1, heads):
                    merged = jnp.where(lane == h, o[h * BLK : (h + 1) * BLK], merged)
                att[layer, span, :] = merged.astype(BF16)
                return carry

            lax.fori_loop(0, qblk, body, 0)

        ac = []
        for r in (2, 1, 0):
            attend(peers[r])
            c = pltpu.make_async_remote_copy(
                att.at[layer, rows_of(peers[r])], arecv.at[layer, r],
                a_send.at[layer, r], a_recv.at[layer, r],
                device_id=dev(dom, peers[r]), device_id_type=MESH,
            )
            c.start()
            ac.append(c)
        attend(m)
        for c in wc[layer, 0] + wc[layer, 2]:
            c.wait_recv()
        y = xrow[...].astype(F32) + mm(att[layer, rows_of(m), :], out_w[layer])
        for c in ac:
            c.wait_recv()
        for r in range(3):
            y = y + mm(arecv[layer, r], gout[layer, r])
        x1 = y.astype(BF16).astype(F32)
        n2 = normalize(x1, ln_gain[2 * layer + 1 : 2 * layer + 2, :]).astype(BF16)
        total = x1 + mm(silu(mm(n2, up_w[layer])).astype(BF16), down_w[layer])
        for r in range(3):
            total = total + mm(silu(mm(n2, gup[layer, r])).astype(BF16), gdown[layer, r])
        xrow[...] = total.astype(BF16)
        pending += ag + halo + ac

    fc = []
    for r in range(3):
        c = pltpu.make_async_remote_copy(
            xrow.at[:, pl.ds(pl.multiple_of(peers[r] * cols, cols), cols)],
            result.at[rows_of(m), :],
            f_send.at[r], f_recv.at[r],
            device_id=dev(dom, peers[r]), device_id_type=MESH,
        )
        c.start()
        fc.append(c)
    result[rows_of(m), :] = xrow[:, mine]
    for k in order:
        for c in started[k]:
            c.wait_send()
    for c in pc + pending:
        c.wait_send()
    for key in wc:
        for c in wc[key]:
            c.wait_send()
    for c in fc:
        c.wait()


def shards(
    grid_feat,
    grid_target,
    enc_w1,
    enc_b1,
    enc_w2,
    enc_gain,
    mesh_embed,
    nbr_blocks,
    attn_bias,
    ln_gain,
    qkv_w,
    out_w,
    up_w,
    down_w,
):
    n_dom = lax.axis_size("dom")
    n_mp = lax.axis_size("mp")
    rows, f_in = grid_feat.shape
    width = enc_w2.shape[1]
    cols = width // n_mp
    nodes = mesh_embed.shape[0]
    local_blocks = nodes // BLK
    heads = cols // HEAD_DIM
    layers = ln_gain.shape[0]
    cap = 2 * rows // n_dom
    quarter = nodes // n_mp
    ff = up_w.shape[2]
    window_start = lax.axis_index("dom") * local_blocks - HB
    slots = ((nbr_blocks - window_start) % (local_blocks * n_dom)).reshape(-1)
    bias = jnp.transpose(
        attn_bias.reshape(heads, NBLK, local_blocks, BLK), (2, 1, 0, 3)
    ).reshape(local_blocks, NBLK, heads * BLK)
    vmem = pl.BlockSpec(memory_space=pltpu.VMEM)
    dma = pltpu.SemaphoreType.DMA
    window = local_blocks + 2 * HB
    return pl.pallas_call(
        functools.partial(mega, n_dom, n_mp, layers),
        out_shape=jax.ShapeDtypeStruct((nodes, cols), BF16),
        in_specs=[pl.BlockSpec(memory_space=pltpu.SMEM)] + [vmem] * 13,
        out_specs=vmem,
        scratch_shapes=[
            pltpu.VMEM((n_dom, cap, f_in), BF16),
            pltpu.VMEM((n_dom, 8, cap), jnp.int32),
            pltpu.VMEM((n_dom, cap, f_in), BF16),
            pltpu.VMEM((n_dom, 8, cap), jnp.int32),
            pltpu.VMEM((nodes, width), F32),
            pltpu.VMEM((3, quarter, width), BF16),
            pltpu.VMEM((3, quarter, width), BF16),
            pltpu.VMEM((quarter, width), BF16),
            pltpu.VMEM((layers, 4, quarter, width), BF16),
            pltpu.VMEM((window, BLK, 2 * cols), BF16),
            pltpu.VMEM((window, BLK, 2 * cols), BF16),
            pltpu.VMEM((layers, nodes, cols), BF16),
            pltpu.VMEM((layers, nodes, cols), BF16),
            pltpu.VMEM((layers, 3, quarter, cols), BF16),
            pltpu.VMEM((layers, 3, cols, width), BF16),
            pltpu.VMEM((layers, 3, width, ff), BF16),
            pltpu.VMEM((layers, 3, ff, width), BF16),
            dma((2, n_dom)),
            dma((2, n_dom)),
            dma((3,)),
            dma((3,)),
            dma((layers, 3)),
            dma((layers, 3)),
            dma((layers, 3, 3)),
            dma((layers, 3, 3)),
            dma((layers, 2)),
            dma((layers, 2)),
            dma((layers, 3)),
            dma((layers, 3)),
            dma((3,)),
            dma((3,)),
        ],
        compiler_params=pltpu.CompilerParams(
            collective_id=0, has_side_effects=True, vmem_limit_bytes=60 * 1024 * 1024
        ),
    )(
        slots,
        grid_feat,
        grid_target.reshape(1, rows),
        enc_w1,
        enc_b1.reshape(1, width),
        enc_w2,
        enc_gain.reshape(1, width),
        mesh_embed,
        bias,
        ln_gain.reshape(2 * layers, width),
        qkv_w,
        out_w,
        up_w,
        down_w,
    )


def solution(mesh):
    placed = (
        P(("dom", "mp"), None),
        P(("dom", "mp")),
        P(),
        P(),
        P(),
        P(),
        P("dom", "mp"),
        P("dom", None),
        P("mp", None, "dom"),
        P(),
        P(None, None, None, "mp"),
        P(None, "mp", None),
        P(None, None, "mp"),
        P(None, "mp", None),
    )
    return jax.shard_map(
        shards, mesh=mesh, in_specs=placed, out_specs=P("dom", "mp"), check_vma=False
    )
```

time: 545 us -> 139 us (0.26)
  the two profiles are of different devices: /device:TPU:13 before, /device:TPU:11 now
where the time goes in v1:
time: 139 us
  Pallas kernels  133 us (96%)
  local copies, waits for them, and re-layouts  5.73 us (4%)
    pallas_call x1, Pallas kernels, shards(): pl.pallas_call(functools.partial(mega, n_dom, n_mp, layers), out_shape=ja...  133 us

profile of v1, /device:TPU:11, one launch (start us, length us, event | category | flops | bytes accessed | tf_op | source)
XLA Modules:
  0.0 138.5 jit_solution(7630137924328669224)
XLA Ops:
  0.0 1.0 reshape.25
  1.0 0.2 copy.17
  1.2 0.8 reshape.26.bias
  2.1 0.0 copy-start
  2.1 0.7 copy-done
  2.8 0.0 copy-start.1
  2.8 0.7 reshape.21.slots
  3.4 0.0 copy-done.1
  3.5 0.6 reshape.27.ln_gain
  4.1 132.8 %shard_map.136 = bf16[1024,128]{1,0:T(8,128)(2,1)} custom-call(s32[256]{0:T(256)} %reshape.21.slots, bf16[1024,256]{1,0:T(8,128)(2,1)} %feat.1, s32[1,1024]{1,0:T(1,128)} %bitcast.7, bf16[256,512]{1,0:T(8,128)(2,1)} %w1.1, f32[1,512]{1,0:T(1,128)} %bitcast.8, bf16[512,512]{1,0:T(8,128)(2,1)} %w2.1, f32[1,512]{1,0:T(1,128)} %bitcast.9, ...), custom_call_target="tpu_custom_call" | custom-call | tf_op jit(solution)/shard_map/pallas_call | solution.py:386
  136.8 1.7 %copy.19 = bf16[1024,128]{1,0:T(8,128)(2,1)} copy(bf16[1024,128]{1,0:T(8,128)(2,1)} %shard_map.136) | data formatting | bytes 524288
  (1 shorter events, 0.0 us)
Async XLA Ops:
  2.1 0.7 copy-start
  2.8 0.7 copy-start.1

commit v2 on v1

--- a/solution.py
+++ b/solution.py
@@ -36,7 +36,7 @@
     n_dom,
     n_mp,
     layers,
-    slots,
+    nbr,
     feat,
     target,
     w1,
@@ -44,13 +44,15 @@
     w2,
     egain,
     embed,
+    bias_in,
+    ln_gain,
+    qkv_hbm,
+    out_hbm,
+    up_hbm,
+    down_hbm,
+    result,
     bias,
-    ln_gain,
     qkv_w,
-    out_w,
-    up_w,
-    down_w,
-    result,
     sbuf,
     sland,
     rbuf,
@@ -82,6 +84,7 @@
     a_recv,
     f_send,
     f_recv,
+    l_sem,
 ):
     dom = lax.axis_index("dom")
     m = lax.axis_index("mp")
@@ -152,9 +155,17 @@
     pl.semaphore_wait(barrier, n_dom - 1 + len(peers))
     started = {}
 
+    weights = ((out_hbm, gout), (up_hbm, gup), (down_hbm, gdown))
+    local = [pltpu.make_async_copy(qkv_hbm, qkv_w, l_sem.at[layers, 0])]
+    for layer in range(layers):
+        for i, (own, got) in enumerate(weights):
+            local.append(
+                pltpu.make_async_copy(own.at[layer], got.at[layer, 3], l_sem.at[layer, i])
+            )
+
     def w_copies(layer, hop):
         out = []
-        for i, (own, got) in enumerate(((out_w, gout), (up_w, gup), (down_w, gdown))):
+        for i, (own, got) in enumerate(weights):
             if hop < 2:
                 src = own.at[layer]
                 p = peers[hop]
@@ -182,7 +193,12 @@
         start_all(started[k])
     start_all(wc[0, 1])
     start_all(wc[0, 0])
+    start_all(local)
     outgoing(0)
+    for b in range(local_blocks):
+        bias[b] = jnp.concatenate(
+            [bias_in[h, :, b * BLK : (b + 1) * BLK] for h in range(heads)], axis=1
+        )
 
     def consume(buf, land, first):
         v = mm(buf, w1[...]) + b1[...]
@@ -198,7 +214,7 @@
     consume(sbuf[0], sland[0], True)
     mine = pl.ds(pl.multiple_of(m * cols, cols), cols)
     acc[:, mine] += embed[...].astype(F32)
-    for k in reversed(order):
+    for k in order:
         for c in started[k]:
             c.wait_recv()
         consume(rbuf[k], rland[k], False)
@@ -206,54 +222,58 @@
     def rows_of(p):
         return pl.ds(pl.multiple_of(p * quarter, quarter), quarter)
 
-    pc = []
-    for r in (2, 1, 0):
-        psend[r] = acc[rows_of(peers[r]), :].astype(BF16)
-        c = pltpu.make_async_remote_copy(
-            psend.at[r], precv.at[r], p_send.at[r], p_recv.at[r],
-            device_id=dev(dom, peers[r]), device_id_type=MESH,
+    def p_copy(i, p):
+        return pltpu.make_async_remote_copy(
+            psend.at[i], precv.at[i], p_send.at[i], p_recv.at[i],
+            device_id=dev(dom, p), device_id_type=MESH,
         )
-        c.start()
-        pc.append(c)
-    total = acc[rows_of(m), :]
-    for c in reversed(pc):
+
+    pc = [p_copy(0, peers[0]), p_copy(1, peers[0]), p_copy(2, peers[1])]
+    psend[0] = acc[rows_of(peers[2]), :].astype(BF16)
+    pc[0].start()
+    psend[1] = acc[rows_of(peers[0]), :].astype(BF16)
+    pc[1].start()
+    pc[0].wait_recv()
+    psend[2] = (acc[rows_of(peers[1]), :] + precv[0].astype(F32)).astype(BF16)
+    pc[2].start()
+    pc[1].wait_recv()
+    total = acc[rows_of(m), :] + precv[1].astype(F32)
+    for c in wc[0, 1]:
         c.wait_recv()
-    for r in range(3):
-        total = total + precv[r].astype(F32)
+    start_all(wc[0, 2])
+    for c in local:
+        c.wait()
+    pc[2].wait_recv()
+    total = total + precv[2].astype(F32)
     xrow[...] = total.astype(BF16)
 
     lane = lax.broadcasted_iota(jnp.int32, (BLK, cols), 1) // HEAD_DIM
+    block_count = local_blocks * n_dom
+
+    def slot_of(b, t):
+        away = nbr[b, t] - (dom * local_blocks - HB)
+        away = jnp.where(away < 0, away + block_count, away)
+        away = jnp.where(away >= block_count, away - block_count, away)
+        return jnp.minimum(away, local_blocks + 2 * HB - 1)
+
     pending = []
     for layer in range(layers):
         kv = (kv0, kv1)[layer]
-        nrm[layer, 3] = normalize(xrow[...].astype(F32), ln_gain[2 * layer : 2 * layer + 1, :]).astype(BF16)
-        ag = []
-        for r in range(3):
-            c = pltpu.make_async_remote_copy(
-                nrm.at[layer, 3], nrm.at[layer, r], ag_send.at[layer, r], ag_recv.at[layer, r],
-                device_id=dev(dom, peers[r]), device_id_type=MESH,
+        nrm[layer, 3] = normalize(xrow[...].astype(F32), ln_gain[layer, 0:1, :]).astype(BF16)
+        half = quarter // 2
+
+        def ag_copy(i, src, dst, part, p):
+            return pltpu.make_async_remote_copy(
+                nrm.at[layer, src, part], nrm.at[layer, dst, part],
+                ag_send.at[layer, i], ag_recv.at[layer, i],
+                device_id=dev(dom, p), device_id_type=MESH,
             )
-            ag.append(c)
-        for r in (2, 1, 0):
-            ag[r].start()
-        if layer + 1 < layers:
-            start_all(wc[layer + 1, 1])
-            start_all(wc[layer + 1, 0])
-
-        def project(r, p):
-            block = nrm[layer, r]
-            q = mm(block, qkv_w[layer, 0]).astype(BF16).astype(F32) * HEAD_DIM ** (-0.5)
-            qs[layer, rows_of(p), :] = q.astype(BF16)
-            spot = pl.ds(HB + p * qblk, qblk)
-            kv[spot, :, 0:cols] = mm(block, qkv_w[layer, 1]).astype(BF16).reshape(qblk, BLK, cols)
-            kv[spot, :, cols : 2 * cols] = (
-                mm(block, qkv_w[layer, 2]).astype(BF16).reshape(qblk, BLK, cols)
-            )
-
-        project(3, m)
-        for r in range(3):
-            ag[r].wait_recv()
-            project(r, peers[r])
+
+        halves = [pl.ds(0, half), pl.ds(half, half)]
+        ag = [ag_copy(1 + i, 3, 1, halves[i], peers[1]) for i in range(2)]
+        ag.append(ag_copy(0, 3, 0, pl.ds(0, quarter), peers[0]))
+        relay = [ag_copy(3 + i, 1, 2, halves[i], peers[0]) for i in range(2)]
+        start_all(ag)
         halo = [
             pltpu.make_async_remote_copy(
                 kv.at[pl.ds(HB, HB)], kv.at[pl.ds(HB + local_blocks, HB)],
@@ -266,10 +286,47 @@
                 device_id=dev((dom + 1) % n_dom, m), device_id_type=MESH,
             ),
         ]
-        start_all(halo)
-        for c in wc[layer, 1]:
+
+        def project(r, p):
+            block = nrm[layer, r]
+            spot = pl.ds(HB + p * qblk, qblk)
+            kv[spot, :, 0:cols] = mm(block, qkv_w[layer, 1]).astype(BF16).reshape(qblk, BLK, cols)
+            kv[spot, :, cols : 2 * cols] = (
+                mm(block, qkv_w[layer, 2]).astype(BF16).reshape(qblk, BLK, cols)
+            )
+
+            @pl.when(p == 0)
+            def _():
+                halo[0].start()
+
+            @pl.when(p == n_mp - 1)
+            def _():
+                halo[1].start()
+
+        def project_q(r, p):
+            q = mm(nrm[layer, r], qkv_w[layer, 0]).astype(BF16).astype(F32) * HEAD_DIM ** (-0.5)
+            qs[layer, rows_of(p), :] = q.astype(BF16)
+
+        project(3, m)
+        ag[2].wait_recv()
+        project(0, peers[0])
+        for i in range(2):
+            ag[i].wait_recv()
+            relay[i].start()
+        project(1, peers[1])
+        for c in relay:
             c.wait_recv()
-        start_all(wc[layer, 2])
+        project(2, peers[2])
+        if layer + 1 < layers:
+            start_all(wc[layer + 1, 1][0:2])
+            start_all(wc[layer + 1, 0][0:2])
+        if layer > 0:
+            for c in wc[layer, 1][0:2]:
+                c.wait_recv()
+            start_all(wc[layer, 2][0:2])
+        project_q(3, m)
+        for r in range(3):
+            project_q(r, peers[r])
         for c in halo:
             c.wait_recv()
 
@@ -281,7 +338,7 @@
                 qbd = jnp.concatenate(
                     [jnp.where(lane == h, q.astype(F32), 0.0) for h in range(heads)], axis=0
                 ).astype(BF16)
-                picked = [kv[slots[b * NBLK + t]] for t in range(NBLK)]
+                picked = [kv[slot_of(b, t)] for t in range(NBLK)]
                 keys = jnp.concatenate([x[:, 0:cols] for x in picked], axis=0)
                 values = jnp.concatenate([x[:, cols : 2 * cols] for x in picked], axis=0)
                 s = lax.dot_general(keys, qbd, (((1,), (1,)), ((), ())), preferred_element_type=F32)
@@ -308,21 +365,28 @@
             )
             c.start()
             ac.append(c)
+        if layer > 0:
+            for c in wc[layer, 1][2:3]:
+                c.wait_recv()
+            start_all(wc[layer, 2][2:3])
         attend(m)
         for c in wc[layer, 0] + wc[layer, 2]:
             c.wait_recv()
-        y = xrow[...].astype(F32) + mm(att[layer, rows_of(m), :], out_w[layer])
+        y = xrow[...].astype(F32) + mm(att[layer, rows_of(m), :], gout[layer, 3])
         for c in ac:
             c.wait_recv()
         for r in range(3):
             y = y + mm(arecv[layer, r], gout[layer, r])
+        if layer + 1 < layers:
+            start_all(wc[layer + 1, 1][2:3])
+            start_all(wc[layer + 1, 0][2:3])
         x1 = y.astype(BF16).astype(F32)
-        n2 = normalize(x1, ln_gain[2 * layer + 1 : 2 * layer + 2, :]).astype(BF16)
-        total = x1 + mm(silu(mm(n2, up_w[layer])).astype(BF16), down_w[layer])
-        for r in range(3):
+        n2 = normalize(x1, ln_gain[layer, 1:2, :]).astype(BF16)
+        total = x1
+        for r in (3, 0, 1, 2):
             total = total + mm(silu(mm(n2, gup[layer, r])).astype(BF16), gdown[layer, r])
         xrow[...] = total.astype(BF16)
-        pending += ag + halo + ac
+        pending += ag + relay + halo + ac
 
     fc = []
     for r in range(3):
@@ -375,20 +439,17 @@
     cap = 2 * rows // n_dom
     quarter = nodes // n_mp
     ff = up_w.shape[2]
-    window_start = lax.axis_index("dom") * local_blocks - HB
-    slots = ((nbr_blocks - window_start) % (local_blocks * n_dom)).reshape(-1)
-    bias = jnp.transpose(
-        attn_bias.reshape(heads, NBLK, local_blocks, BLK), (2, 1, 0, 3)
-    ).reshape(local_blocks, NBLK, heads * BLK)
     vmem = pl.BlockSpec(memory_space=pltpu.VMEM)
     dma = pltpu.SemaphoreType.DMA
     window = local_blocks + 2 * HB
     return pl.pallas_call(
         functools.partial(mega, n_dom, n_mp, layers),
         out_shape=jax.ShapeDtypeStruct((nodes, cols), BF16),
-        in_specs=[pl.BlockSpec(memory_space=pltpu.SMEM)] + [vmem] * 13,
+        in_specs=[pl.BlockSpec(memory_space=pltpu.SMEM)] + [vmem] * 9 + [pl.BlockSpec(memory_space=pl.ANY)] * 4,
         out_specs=vmem,
         scratch_shapes=[
+            pltpu.VMEM((local_blocks, NBLK, heads * BLK), F32),
+            pltpu.VMEM(qkv_w.shape, BF16),
             pltpu.VMEM((n_dom, cap, f_in), BF16),
             pltpu.VMEM((n_dom, 8, cap), jnp.int32),
             pltpu.VMEM((n_dom, cap, f_in), BF16),
@@ -403,15 +464,15 @@
             pltpu.VMEM((layers, nodes, cols), BF16),
             pltpu.VMEM((layers, nodes, cols), BF16),
             pltpu.VMEM((layers, 3, quarter, cols), BF16),
-            pltpu.VMEM((layers, 3, cols, width), BF16),
-            pltpu.VMEM((layers, 3, width, ff), BF16),
-            pltpu.VMEM((layers, 3, ff, width), BF16),
+            pltpu.VMEM((layers, 4, cols, width), BF16),
+            pltpu.VMEM((layers, 4, width, ff), BF16),
+            pltpu.VMEM((layers, 4, ff, width), BF16),
             dma((2, n_dom)),
             dma((2, n_dom)),
             dma((3,)),
             dma((3,)),
-            dma((layers, 3)),
-            dma((layers, 3)),
+            dma((layers, 5)),
+            dma((layers, 5)),
             dma((layers, 3, 3)),
             dma((layers, 3, 3)),
             dma((layers, 2)),
@@ -420,12 +481,13 @@
             dma((layers, 3)),
             dma((3,)),
             dma((3,)),
+            dma((layers + 1, 3)),
         ],
         compiler_params=pltpu.CompilerParams(
             collective_id=0, has_side_effects=True, vmem_limit_bytes=60 * 1024 * 1024
         ),
     )(
-        slots,
+        nbr_blocks,
         grid_feat,
         grid_target.reshape(1, rows),
         enc_w1,
@@ -433,8 +495,8 @@
         enc_w2,
         enc_gain.reshape(1, width),
         mesh_embed,
-        bias,
-        ln_gain.reshape(2 * layers, width),
+        attn_bias,
+        ln_gain,
         qkv_w,
         out_w,
         up_w,

time: 139 us -> 119 us (0.86)
  the two profiles are of different devices: /device:TPU:11 before, /device:TPU:13 now
where the time goes in v2:
time: 119 us
  Pallas kernels  118 us (99%)
  local copies, waits for them, and re-layouts  1.67 us (1%)
    pallas_call x1, Pallas kernels, shards(): pl.pallas_call(functools.partial(mega, n_dom, n_mp, layers), out_shape=ja...  118 us

profile of v2, /device:TPU:13, one launch (start us, length us, event | category | flops | bytes accessed | tf_op | source)
XLA Modules:
  0.0 119.3 jit_solution(9002725400937789864)
XLA Ops:
  0.0 117.6 %shard_map.136 = bf16[1024,128]{1,0:T(8,128)(2,1)} custom-call(s32[16,16]{1,0:T(8,128)} %nbr.1, bf16[1024,256]{1,0:T(8,128)(2,1)} %feat.1, s32[1,1024]{1,0:T(1,128)} %bitcast.3, bf16[256,512]{1,0:T(8,128)(2,1)} %w1.1, f32[1,512]{1,0:T(1,128)} %bitcast.4, bf16[512,512]{1,0:T(8,128)(2,1)} %w2.1, f32[1,512]{1,0:T(1,128)} %bitcast.5, bf16[1024,128]{1,0:T(8,128)(2,1)} %embed.1, ...), custom_call_target="tpu_custom_call" | custom-call | tf_op jit(solution)/shard_map/pallas_call | solution.py:445
  117.6 1.7 %copy.16 = bf16[1024,128]{1,0:T(8,128)(2,1)} copy(bf16[1024,128]{1,0:T(8,128)(2,1)} %shard_map.136) | data formatting | bytes 524288

commit v3 on v2

--- a/solution.py
+++ b/solution.py
@@ -370,12 +370,11 @@
                 c.wait_recv()
             start_all(wc[layer, 2][2:3])
         attend(m)
-        for c in wc[layer, 0] + wc[layer, 2]:
+        for c in wc[layer, 0][0:1] + wc[layer, 2][0:1]:
             c.wait_recv()
         y = xrow[...].astype(F32) + mm(att[layer, rows_of(m), :], gout[layer, 3])
-        for c in ac:
+        for c, r in zip(ac, (2, 1, 0)):
             c.wait_recv()
-        for r in range(3):
             y = y + mm(arecv[layer, r], gout[layer, r])
         if layer + 1 < layers:
             start_all(wc[layer + 1, 1][2:3])
@@ -383,7 +382,10 @@
         x1 = y.astype(BF16).astype(F32)
         n2 = normalize(x1, ln_gain[layer, 1:2, :]).astype(BF16)
         total = x1
-        for r in (3, 0, 1, 2):
+        for r in (3, 1, 0, 2):
+            if r in (0, 2):
+                for c in wc[layer, r][1:3]:
+                    c.wait_recv()
             total = total + mm(silu(mm(n2, gup[layer, r])).astype(BF16), gdown[layer, r])
         xrow[...] = total.astype(BF16)
         pending += ag + relay + halo + ac

time: 119 us -> 120 us (level)
  no operation moved by 1% of the time
where the time goes in v3:
time: 120 us; the launch traced here: 119 us
  Pallas kernels  118 us (98%)
  local copies, waits for them, and re-layouts  1.67 us (1%)
    pallas_call x1, Pallas kernels, shards(): pl.pallas_call(functools.partial(mega, n_dom, n_mp, layers), out_shape=ja...  118 us

profile of v3, /device:TPU:13, one launch (start us, length us, event | category | flops | bytes accessed | tf_op | source)
XLA Modules:
  0.0 119.4 jit_solution(18353816969738323524)
XLA Ops:
  0.0 117.7 %shard_map.136 = bf16[1024,128]{1,0:T(8,128)(2,1)} custom-call(s32[16,16]{1,0:T(8,128)} %nbr.1, bf16[1024,256]{1,0:T(8,128)(2,1)} %feat.1, s32[1,1024]{1,0:T(1,128)} %bitcast.3, bf16[256,512]{1,0:T(8,128)(2,1)} %w1.1, f32[1,512]{1,0:T(1,128)} %bitcast.4, bf16[512,512]{1,0:T(8,128)(2,1)} %w2.1, f32[1,512]{1,0:T(1,128)} %bitcast.5, bf16[1024,128]{1,0:T(8,128)(2,1)} %embed.1, ...), custom_call_target="tpu_custom_call" | custom-call | tf_op jit(solution)/shard_map/pallas_call | solution.py:447
  117.7 1.7 %copy.16 = bf16[1024,128]{1,0:T(8,128)(2,1)} copy(bf16[1024,128]{1,0:T(8,128)(2,1)} %shard_map.136) | data formatting | bytes 524288
